TPU v7x, 32 devices: a whole 2x2x4 slice. The times are simulated.
32 devices in a mesh: grp: 4 (over x, core), own: 8 (over z, y).
Axes of the slice: x: 2, y: 2, z: 4, core: 2. Of those that a mesh axis runs over, the one named last changes fastest.
Arguments:
- orbitals: bfloat16 [32, 32, 1024], P(('grp', 'own')), may hold values from -3 to 3
- offsets: int32 [32, 2], P(('grp', 'own')), may hold values from 0 to 32
- pairs: int32 [32, 2], P('grp'), may hold values from 0 to 7, as said below
- ext_pot: bfloat16 [32, 4096], replicated, may hold values from -6 to 6
Outputs:
- gradient: float32 [32, 32, 1024], P(('grp', 'own'))
Inputs may be any that keep to these rules, and one draw needn't show every extreme that they name: `pairs`: rows g * 8 to g * 8 + 7 belong to group g; each row names two different orbitals of the group. Calling owner o the device holding orbital o of a group, at most 2 rows of a group have orbital o as their first orbital, and in every group some owner has exactly 2.
All inputs are finite; a program needn't handle non-finite values.
Results may differ from a plain program's by a relative error of at most 0.0006.
Values may be sent and summed in bfloat16 or wider, within the bound.
A program may use at most 64 MiB of HBM per device.

v0:
```python
import functools
import math

import jax
import jax.numpy as jnp
from jax import lax
from jax.experimental import pallas as pl
from jax.experimental.pallas import tpu as pltpu
from jax.sharding import PartitionSpec as P

SCREEN = 0.0025
MIXING = 0.25
EXCHANGE_COEF = (3.0 / math.pi) ** (1.0 / 3.0)
PRECISE = lax.Precision.HIGHEST
VMEM = pltpu.VMEM


def side_of(cells):
    return math.isqrt(cells)


def cas_table(length, count):
    row = lax.broadcasted_iota(jnp.int32, (length, count), 0)
    col = lax.broadcasted_iota(jnp.int32, (length, count), 1)
    angle = 2.0 * math.pi / length * (row * col % length).astype(jnp.float32)
    return jnp.cos(angle) + jnp.sin(angle)


def wave_squares(length):
    positions = jnp.arange(length, dtype=jnp.int32)
    signed = jnp.where(positions < length // 2, positions, positions - length)
    wavenumber = 2.0 * math.pi / length * signed.astype(jnp.float32)
    return wavenumber * wavenumber


def green_table(depth, width):
    along_z = wave_squares(2 * depth)
    along_y = wave_squares(2 * width)
    squared_sum = along_z[:, None, None] + along_y[None, :, None] + along_y[None, None, :]
    return 4.0 * math.pi / (squared_sum + SCREEN)


def rotate(pattern, matrix, operand):
    return jnp.einsum(pattern, matrix, operand, precision=PRECISE, preferred_element_type=jnp.float32)


def poisson_solve(density, transforms):
    green_values, along_z, along_y = transforms
    value = rotate("kz,zyx->kyx", along_z, density)
    value = rotate("ky,zyx->zkx", along_y, value)
    value = rotate("kx,zyx->zyk", along_y, value)
    value = value * green_values
    value = rotate("kx,zyk->zyx", along_y, value)
    value = rotate("ky,zkx->zyx", along_y, value)
    return rotate("kz,kyx->zyx", along_z, value)


def shifted(box_data, shift_y, shift_x):
    depth, side, _ = box_data.shape
    padded = jnp.pad(box_data, ((0, 0), (side, side), (side, side)))
    anchor = jnp.zeros((), jnp.int32)
    corner = (anchor, (side + shift_y).astype(jnp.int32), (side + shift_x).astype(jnp.int32))
    return lax.dynamic_slice(padded, corner, (depth, side, side))


def placer(starts, row_count, side):
    grid_index = lax.broadcasted_iota(jnp.int32, (starts.shape[0], row_count, side), 1)
    cell_index = lax.broadcasted_iota(jnp.int32, (starts.shape[0], row_count, side), 2)
    return (grid_index == cell_index + starts[:, None, None]).astype(jnp.float32)


def greet(axis, count):
    me = lax.axis_index(axis)
    barrier = pltpu.get_barrier_semaphore()

    def hello(step, carry):
        peer = lax.rem(me + step, count)
        pl.semaphore_signal(barrier, inc=1, device_id={axis: peer}, device_id_type=pl.DeviceIdType.MESH)
        return carry

    lax.fori_loop(1, count, hello, 0)
    pl.semaphore_wait(barrier, count - 1)


def gather_kernel(axis, count, *refs):
    pieces = (len(refs) - 3) // 2
    sources, targets = refs[:pieces], refs[pieces : 2 * pieces]
    send_sem, recv_sem, local_sem = refs[2 * pieces :]
    me = lax.axis_index(axis)
    greet(axis, count)

    def copy_to(piece, step):
        return pltpu.make_async_remote_copy(
            src_ref=sources[piece],
            dst_ref=targets[piece].at[me],
            send_sem=send_sem.at[piece, step],
            recv_sem=recv_sem.at[piece, step],
            device_id={axis: lax.rem(me + step, count)},
            device_id_type=pl.DeviceIdType.MESH,
        )

    for step in range(1, count):
        for piece in range(pieces):
            copy_to(piece, step).start()
    for piece in range(pieces):
        own = pltpu.make_async_copy(sources[piece], targets[piece].at[me], local_sem.at[piece])
        own.start()
        own.wait()
    for step in range(1, count):
        for piece in range(pieces):
            copy_to(piece, step).wait()


def gather(axis, count, collective_id, *arrays):
    pieces = len(arrays)
    return pl.pallas_call(
        functools.partial(gather_kernel, axis, count),
        out_shape=[jax.ShapeDtypeStruct((count,) + a.shape, a.dtype) for a in arrays],
        in_specs=[pl.BlockSpec(memory_space=VMEM)] * pieces,
        out_specs=[pl.BlockSpec(memory_space=VMEM)] * pieces,
        scratch_shapes=[
            pltpu.SemaphoreType.DMA((pieces, count)),
            pltpu.SemaphoreType.DMA((pieces, count)),
            pltpu.SemaphoreType.DMA((pieces,)),
        ],
        compiler_params=pltpu.CompilerParams(collective_id=collective_id, has_side_effects=True),
        name="gather_" + axis,
    )(*arrays)


def return_kernel(axis, count, terms, read, phi, out, term_slots, read_slots, send_sem, recv_sem):
    me = lax.axis_index(axis)
    depth = read.shape[1]
    greet(axis, count)

    def copies(step):
        peer = lax.rem(me + step, count)
        pair = []
        for piece, (source, slots) in enumerate(((terms, term_slots), (read, read_slots))):
            pair.append(
                pltpu.make_async_remote_copy(
                    src_ref=source.at[peer],
                    dst_ref=slots.at[me],
                    send_sem=send_sem.at[piece, step],
                    recv_sem=recv_sem.at[piece, step],
                    device_id={axis: peer},
                    device_id_type=pl.DeviceIdType.MESH,
                )
            )
        return pair

    for step in range(1, count):
        for copy in copies(step):
            copy.start()
    total = terms[me]
    for step in range(1, count):
        for copy in copies(step):
            copy.wait()
        total = total + term_slots[lax.rem(me + count - step, count)]
    read_slots[me] = read[me]
    for owner in range(count):
        rows = slice(owner * depth, (owner + 1) * depth)
        out[rows, :] = read_slots[owner] * phi[rows, :] - MIXING * total[rows, :]


def send_back(axis, count, collective_id, terms, read, phi):
    return pl.pallas_call(
        functools.partial(return_kernel, axis, count),
        out_shape=jax.ShapeDtypeStruct(phi.shape, jnp.float32),
        in_specs=[pl.BlockSpec(memory_space=VMEM)] * 3,
        out_specs=pl.BlockSpec(memory_space=VMEM),
        scratch_shapes=[
            VMEM(terms.shape, jnp.float32),
            VMEM(read.shape, jnp.float32),
            pltpu.SemaphoreType.DMA((2, count)),
            pltpu.SemaphoreType.DMA((2, count)),
        ],
        compiler_params=pltpu.CompilerParams(collective_id=collective_id, has_side_effects=True),
        name="send_back",
    )(terms, read, phi)


def body(owners, groups, orbitals, offsets, pairs, ext_pot):
    owner = lax.axis_index("own")
    _, levels, cells = orbitals.shape
    side = side_of(cells)
    grid = side_of(ext_pot.shape[1])
    depth = levels // owners
    padded = jnp.pad(offsets, ((0, 7), (0, 126)))
    boxes, spread = gather("own", owners, 0, orbitals[0], padded)
    corners = spread[:, 0, :2]

    planes = lax.dynamic_slice_in_dim(boxes, owner * depth, depth, 1).astype(jnp.float32)
    planes = planes.reshape(owners, depth, side, side)
    along_rows = placer(corners[:, 0], grid, side)
    along_cols = placer(corners[:, 1], grid, side)
    partial = jnp.einsum("izyx,ihx->izyh", planes * planes, along_cols, precision=PRECISE)
    partial = jnp.einsum("igy,izyh->zgh", along_rows, partial, precision=PRECISE)
    (shares,) = gather("grp", groups, 1, partial.reshape(depth, grid * grid))
    density = jnp.sum(shares, axis=0)
    external = lax.dynamic_slice_in_dim(ext_pot, owner * depth, depth, 0)
    potential = external.astype(jnp.float32) - EXCHANGE_COEF * jnp.cbrt(density)
    potential = potential.reshape(depth, grid, grid)
    read = jnp.einsum("igy,zgh->izyh", along_rows, potential, precision=PRECISE)
    read = jnp.einsum("izyh,ihx->izyx", read, along_cols, precision=PRECISE)
    read = read.reshape(owners, depth, cells)

    transforms = (
        green_table(levels, side) * (1.0 / float(8 * levels * cells)),
        cas_table(2 * levels, levels),
        cas_table(2 * side, side),
    )
    terms = jnp.zeros((owners, levels, cells), jnp.float32)
    each = pairs.shape[0] // owners
    slots = jnp.arange(owners, dtype=jnp.int32)
    for turn in range(each):
        first = pairs[owner * each + turn, 0]
        second = pairs[owner * each + turn, 1]
        shift = corners[second] - corners[first]
        near = boxes[first].astype(jnp.float32).reshape(levels, side, side)
        far = boxes[second].astype(jnp.float32).reshape(levels, side, side)
        moved = shifted(far, -shift[0], -shift[1])
        field = poisson_solve(near * moved, transforms)
        to_first = (field * moved).reshape(levels, cells)
        to_second = shifted(field * near, shift[0], shift[1]).reshape(levels, cells)
        terms = terms + jnp.where((slots == first)[:, None, None], to_first, 0.0)
        terms = terms + jnp.where((slots == second)[:, None, None], to_second, 0.0)
    gradient = send_back("own", owners, 2, terms, read, orbitals[0].astype(jnp.float32))
    return gradient[None]


def solution(mesh):
    in_specs = (P(("grp", "own"), None, None), P(("grp", "own"), None), P("grp", None), P())
    out_specs = P(("grp", "own"), None, None)
    run = functools.partial(body, mesh.shape["own"], mesh.shape["grp"])
    return jax.shard_map(run, mesh=mesh, in_specs=in_specs, out_specs=out_specs, check_vma=False)
```

profile of v0, /device:TPU:15, one launch (start us, length us, event | category | flops | bytes accessed | tf_op | source)
XLA Modules:
  0.0 101.8 jit_solution(17997279337119790595)
XLA Ops:
  0.0 1.3 %constant_dynamic-slice_fusion.3 = (s32[1,1]{0,1:T(1,128)}, s32[1,1]{0,1:T(1,128)}) fusion(s32[8,2]{0,1:T(2,128)} %param.6, s32[]{:T(128)S(6)} %select_n.71), kind=kLoop, calls=%fused_computation.69 | loop fusion | bytes 20 | tf_op jit(solution)/shard_map/dynamic_slice | solution.py:217
  5.2 1.3 %iota_compare_fusion = (pred[8]{0:T(512)(128)(4,1)S(1)}, pred[8]{0:T(512)(128)(4,1)S(1)}) fusion(s32[]{:T(128)} %bitcast.3, s32[]{:T(128)} %bitcast), kind=kLoop, calls=%fused_computation.76 | loop fusion | flops 16 | bytes 24 | tf_op jit(solution)/shard_map/eq | solution.py:227
  6.4 1.3 %pad.14.refs_1_ = s32[8,128]{1,0:T(8,128)} pad(s32[1,2]{1,0:T(1,128)} %param.5, s32[]{:T(128)} %constant.59.clone.1), padding=0_7x0_126 | pad | bytes 4108 | tf_op jit(solution)/shard_map/jit(_pad)/pad | solution.py:189
  7.8 1.5 %bitcast_convert_fusion.phi = f32[32,1024]{1,0:T(8,128)} fusion(bf16[1,32,1024]{2,1,0:T(8,128)(2,1)} %param.4), kind=kLoop, calls=%fused_computation.79 | loop fusion | flops 32768 | bytes 196608 | tf_op jit(solution)/shard_map/convert_element_type | solution.py:228
  9.3 18.6 %gather_own.1 = (bf16[8,32,1024]{2,1,0:T(8,128)(2,1)}, s32[8,8,128]{2,1,0:T(8,128)}) custom-call(bf16[32,1024]{1,0:T(8,128)(2,1)} %bitcast.70, s32[8,128]{1,0:T(8,128)} %pad.14.refs_1_), custom_call_target="tpu_custom_call" | custom-call | tf_op jit(solution)/shard_map/gather_own/pallas_call | solution.py:116
  27.8 0.8 slice.19
  33.2 1.0 convert_multiply_fusion.3
  34.2 0.9 constant_dynamic-slice_fusion.2
  36.7 0.7 reshape.153.refs_0_
  37.5 7.2 %gather_grp.1 = f32[4,4,4096]{2,1,0:T(4,128)} custom-call(f32[4,4096]{1,0:T(4,128)} %reshape.153.refs_0_), custom_call_target="tpu_custom_call" | custom-call | tf_op jit(solution)/shard_map/gather_grp/pallas_call | solution.py:116
  44.7 1.0 reduce_sum.9
  45.7 1.0 multiply_subtract_fusion
  47.7 0.9 reshape.155.read
  48.7 1.4 %fusion.11 = f32[64,32,32]{0,2,1:T(8,128)S(1)} fusion(f32[32,32,32]{2,1,0:T(8,128)S(1)} %reshape.156, s32[]{:T(128)S(6)} %select_n.75, s32[]{:T(128)S(6)} %select_n.76, bf16[32,32,32]{2,0,1:T(8,128)(2,1)S(1)} %copy.9), kind=kOutput, calls=%fused_computation.19 | convolution fusion | flops 25262080 | bytes 458760 | tf_op jit(solution)/shard_map/kz,zyx->kyx/dot_general | solution.py:44
  50.2 0.9 copy.16
  51.1 1.8 %convolution_bitcast_fusion = f32[64,64,32]{1,2,0:T(8,128)S(1)} fusion(f32[64,32,32]{2,1,0:T(8,128)S(1)} %copy.16), kind=kOutput, calls=%fused_computation.7 | convolution fusion | flops 50362368 | bytes 786432 | tf_op jit(solution)/shard_map/ky,zyx->zkx/dot_general | solution.py:44
  52.9 3.5 %fusion.37 = f32[64,64,64]{2,1,0:T(8,128)S(1)} fusion(f32[64,64,32]{1,2,0:T(8,128)S(1)} %convolution_bitcast_fusion), kind=kOutput, calls=%fused_computation.50 | convolution fusion | flops 100694016 | bytes 1572864 | tf_op jit(solution)/shard_map/kx,zyx->zyk/dot_general | solution.py:44
  56.4 2.2 %fusion = f32[64,64,32]{2,1,0:T(8,128)S(1)} fusion(f32[64,64,64]{2,1,0:T(8,128)S(1)} %fusion.37, f32[64]{0:T(128)S(1)} %fusion.53, f32[64,64]{1,0:T(8,128)S(1)} %broadcast_add_fusion), kind=kOutput, calls=%fused_computation | convolution fusion | flops 102004736 | bytes 1589504 | tf_op jit(solution)/shard_map/kx,zyk->zyx/dot_general | solution.py:44
  58.6 3.6 %fusion.34 = f32[64,32,32]{2,1,0:T(8,128)S(1)} fusion(f32[64,64,32]{2,1,0:T(8,128)S(1)} %fusion), kind=kOutput, calls=%fused_computation.47 | convolution fusion | flops 50362368 | bytes 786432 | tf_op jit(solution)/shard_map/ky,zkx->zyx/dot_general | solution.py:44
  62.2 0.8 copy.17
  63.0 2.6 %convert_multiply_fusion.1 = (f32[32,32,32]{2,0,1:T(8,128)S(1)}, f32[32,32,32]{2,0,1:T(8,128)S(1)}) fusion(s32[]{:T(128)S(6)} %select_n.75, s32[]{:T(128)S(6)} %select_n.76, bf16[32,32,32]{2,0,1:T(8,128)(2,1)S(1)} %copy.9, f32[32,32,32]{2,1,0:T(8,128)S(1)} %reshape.156, f32[64,32,32]{0,1,2:T(8,128)S(1)} %copy.17), kind=kOutput, calls=%fused_computation.18 | convolution fusion | flops 25294848 | bytes 720904 | tf_op jit(solution)/shard_map/kz,kyx->zyx/dot_general | solution.py:44
  67.1 1.2 %select_add_fusion.terms = f32[8,32,1024]{2,1,0:T(8,128)} fusion(f32[32,1024]{1,0:T(8,128)S(1)} %reshape.152, f32[32,1024]{1,0:T(8,128)S(1)} %reshape.151, pred[8]{0:T(512)(128)(4,1)S(1)} %get-tuple-element.19, pred[8]{0:T(512)(128)(4,1)S(1)} %get-tuple-element.20), kind=kLoop, calls=%fused_computation.10 | loop fusion | flops 786432 | bytes 1310736 | tf_op jit(solution)/shard_map/add | solution.py:227
  68.3 31.9 %send_back.1 = f32[32,1024]{1,0:T(8,128)} custom-call(f32[8,32,1024]{2,1,0:T(8,128)} %select_add_fusion.terms, f32[8,4,1024]{2,1,0:T(4,128)} %reshape.155.read, f32[32,1024]{1,0:T(8,128)} %bitcast_convert_fusion.phi), custom_call_target="tpu_custom_call" | custom-call | tf_op jit(solution)/shard_map/send_back/pallas_call | solution.py:167
  100.2 1.6 %copy.30 = f32[1,32,1024]{2,1,0:T(8,128)} copy(f32[1,32,1024]{2,1,0:T(8,128)} %bitcast.69) | data formatting | bytes 262144
  (21 shorter events, 4.9 us)
where the time goes:
time: 102 us
  Pallas kernels  57.7 us (57%)
  matrix products  17 us (17%)
  local copies, waits for them, and re-layouts  11.2 us (11%)
  between operations  7.96 us (8%)
  other arithmetic  7.87 us (8%)
    pallas_call x1, Pallas kernels, send_back(): pl.pallas_call(functools.partial(return_kernel, axis, count), out_shape=j...  31.9 us
    pallas_call x2, Pallas kernels, gather(): pl.pallas_call(functools.partial(gather_kernel, axis, count), out_shape=[...  25.8 us
    dot_general x6, matrix products, rotate(): jnp.einsum(pattern, matrix, operand, precision=PRECISE, preferred_element...  15.1 us

commit v1 on v0

v1 whole, which is shorter than its diff:
```python
import functools
import math

import jax
import jax.numpy as jnp
from jax import lax
from jax.experimental import pallas as pl
from jax.experimental.pallas import tpu as pltpu
from jax.sharding import PartitionSpec as P

SCREEN = 0.0025
MIXING = 0.25
EXCHANGE_COEF = (3.0 / math.pi) ** (1.0 / 3.0)
PRECISE = lax.Precision.HIGHEST
VMEM = pltpu.VMEM


def side_of(cells):
    return math.isqrt(cells)


def cas_table(length, count):
    row = lax.broadcasted_iota(jnp.int32, (length, count), 0)
    col = lax.broadcasted_iota(jnp.int32, (length, count), 1)
    angle = 2.0 * math.pi / length * (row * col % length).astype(jnp.float32)
    return jnp.cos(angle) + jnp.sin(angle)


def wave_squares(length):
    positions = jnp.arange(length, dtype=jnp.int32)
    signed = jnp.where(positions < length // 2, positions, positions - length)
    wavenumber = 2.0 * math.pi / length * signed.astype(jnp.float32)
    return wavenumber * wavenumber


def green_table(depth, width):
    along_z = wave_squares(2 * depth)
    along_y = wave_squares(2 * width)
    squared_sum = along_z[:, None, None] + along_y[None, :, None] + along_y[None, None, :]
    return 4.0 * math.pi / (squared_sum + SCREEN)


def rotate(pattern, matrix, operand):
    return jnp.einsum(pattern, matrix, operand, precision=PRECISE, preferred_element_type=jnp.float32)


def placer(starts, row_count, side):
    grid_index = lax.broadcasted_iota(jnp.int32, (starts.shape[0], row_count, side), 1)
    cell_index = lax.broadcasted_iota(jnp.int32, (starts.shape[0], row_count, side), 2)
    return (grid_index == cell_index + starts[:, None, None]).astype(jnp.float32)


def plane_split(count):
    rows = 1 << ((count.bit_length() - 1) // 2)
    return count // rows, rows


def relay_kernel(count, pieces, exchanged, *refs):
    far, near = plane_split(count)
    sources, slabs = refs[:pieces], refs[pieces : pieces + exchanged]
    refs = refs[pieces + exchanged :]
    targets, landings = refs[:pieces], refs[pieces : pieces + exchanged]
    send_sem, recv_sem, local_sem, slab_send, slab_recv = refs[pieces + exchanged :]
    me = lax.axis_index("own")
    z = me // near
    y = lax.rem(me, near)
    barrier = pltpu.get_barrier_semaphore()

    def across(step):
        return z * near + lax.rem(y + step, near)

    def signal(peer):
        pl.semaphore_signal(barrier, inc=1, device_id={"own": peer}, device_id_type=pl.DeviceIdType.MESH)

    if exchanged:
        for step in range(1, count):
            signal(lax.rem(me + step, count))
        pl.semaphore_wait(barrier, count - 1)
    else:
        for step in range(1, near):
            signal(across(step))
        pl.when(z > 0)(lambda: signal(me - near))
        pl.when(z < far - 1)(lambda: signal(me + near))
        pl.semaphore_wait(barrier, near - 1 + (z > 0).astype(jnp.int32) + (z < far - 1).astype(jnp.int32))

    parts = []
    for piece, source in enumerate(sources):
        rows = source.shape[0]
        if piece == 0:
            parts.append((piece, 0, rows // 2, False))
            parts.append((piece, rows // 2, rows // 2, True))
        else:
            parts.append((piece, 0, rows, True))
    fronts = [i for i, part in enumerate(parts) if not part[3]]
    backs = [i for i, part in enumerate(parts) if part[3]]

    def copy(index, origin, lane, peer, own):
        piece, start, size, _ = parts[index]
        rows = pl.ds(start, size)
        source = sources[piece].at[rows] if own else targets[piece].at[origin, rows]
        return pltpu.make_async_remote_copy(
            src_ref=source,
            dst_ref=targets[piece].at[origin, rows],
            send_sem=send_sem.at[index, origin, lane],
            recv_sem=recv_sem.at[index, origin],
            device_id={"own": peer},
            device_id_type=pl.DeviceIdType.MESH,
        )

    def slab_copy(index, step):
        peer = lax.rem(me + step, count)
        return pltpu.make_async_remote_copy(
            src_ref=slabs[index].at[peer],
            dst_ref=landings[index].at[me],
            send_sem=slab_send.at[index, step],
            recv_sem=slab_recv.at[index, step],
            device_id={"own": peer},
            device_id_type=pl.DeviceIdType.MESH,
        )

    def both(index, origin, own, act):
        pl.when(z < far - 1)(lambda: act(copy(index, origin, 0, me + near, own)))
        pl.when(z > 0)(lambda: act(copy(index, origin, 1, me - near, own)))

    def sideways(index, origin, own, act):
        for step in range(1, near):
            act(copy(index, origin, 1 + step, across(step), own))

    def start(item):
        item.start()

    def sent(item):
        item.wait_send()

    def arrived(index, origin):
        copy(index, origin, 0, me, False).wait_recv()

    for index in backs:
        both(index, me, True, start)
    for index in fronts:
        sideways(index, me, True, start)
    for index in backs:
        sideways(index, me, True, start)
    for index in range(exchanged):
        for step in range(1, count):
            slab_copy(index, step).start()
    for index in fronts:
        both(index, me, True, start)
    locals_ = [
        pltpu.make_async_copy(sources[piece], targets[piece].at[me], local_sem.at[piece]) for piece in range(pieces)
    ]
    for index in range(exchanged):
        locals_.append(pltpu.make_async_copy(slabs[index].at[me], landings[index].at[me], local_sem.at[pieces + index]))
    for item in locals_:
        item.start()
    for step in range(1, near):
        for index in fronts:
            arrived(index, across(step))
            both(index, across(step), False, start)

    def hop(distance, direction):
        here = z - direction * distance
        inside = (here >= 0) & (here < far)
        onward = inside & (z + direction >= 0) & (z + direction < far)
        lane = 0 if direction > 0 else 1
        neighbour = me + direction * near
        return here, inside, onward, lane, neighbour

    def travel(act, receive):
        for distance in range(1, far):
            for direction in (1, -1):
                here, inside, onward, lane, neighbour = hop(distance, direction)
                for index in backs:
                    origin = here * near + y
                    if receive:
                        pl.when(inside)(functools.partial(arrived, index, origin))
                    pl.when(onward)(lambda: act(copy(index, origin, lane, neighbour, False)))
                    pl.when(inside)(lambda: sideways(index, origin, False, act))
                for index in fronts:
                    for step in range(near):
                        origin = here * near + lax.rem(y + step, near)
                        if receive:
                            pl.when(inside)(functools.partial(arrived, index, origin))
                        pl.when(onward)(lambda: act(copy(index, origin, lane, neighbour, False)))

    travel(start, True)
    for level in range(far):
        for step in range(1, near):
            for index in backs:
                arrived(index, level * near + lax.rem(y + step, near))
    for index in range(exchanged):
        for step in range(1, count):
            slab_copy(index, step).wait()
    for index in backs + fronts:
        both(index, me, True, sent)
        sideways(index, me, True, sent)
    for step in range(1, near):
        for index in fronts:
            both(index, across(step), False, sent)
    travel(sent, False)
    for item in locals_:
        item.wait()


def relay(count, collective_id, arrays, slabs=()):
    pieces, exchanged = len(arrays), len(slabs)
    _, near = plane_split(count)
    shapes = [jax.ShapeDtypeStruct((count,) + a.shape, a.dtype) for a in arrays]
    shapes += [jax.ShapeDtypeStruct(a.shape, a.dtype) for a in slabs]
    return pl.pallas_call(
        functools.partial(relay_kernel, count, pieces, exchanged),
        out_shape=shapes,
        in_specs=[pl.BlockSpec(memory_space=VMEM)] * (pieces + exchanged),
        out_specs=[pl.BlockSpec(memory_space=VMEM)] * (pieces + exchanged),
        scratch_shapes=[
            pltpu.SemaphoreType.DMA((pieces + 1, count, near + 1)),
            pltpu.SemaphoreType.DMA((pieces + 1, count)),
            pltpu.SemaphoreType.DMA((pieces + exchanged,)),
            pltpu.SemaphoreType.DMA((max(exchanged, 1), count)),
            pltpu.SemaphoreType.DMA((max(exchanged, 1), count)),
        ],
        compiler_params=pltpu.CompilerParams(collective_id=collective_id, has_side_effects=True),
        name="relay",
    )(*arrays, *slabs)


def slide(value, shift_y, shift_x, side):
    cells = value.shape[1]
    lane = lax.broadcasted_iota(jnp.int32, value.shape, 1)
    y = lane // side - shift_y
    x = lax.rem(lane, side) - shift_x
    inside = (y >= 0) & (y < side) & (x >= 0) & (x < side)
    amount = lax.rem(shift_y * side + shift_x + 2 * cells, cells)
    return jnp.where(inside, pltpu.roll(value, amount, axis=1), 0.0)


def pair_kernel(each, side, owner_ref, pairs, corners, boxes, rho):
    base = owner_ref[0] * each
    for turn in range(each):
        first, second = pairs[base + turn, 0], pairs[base + turn, 1]
        dy = corners[second, 0] - corners[first, 0]
        dx = corners[second, 1] - corners[first, 1]
        moved = slide(boxes[second].astype(jnp.float32), dy, dx, side)
        rho[turn] = boxes[first].astype(jnp.float32) * moved


def combine_kernel(side, owner_ref, pairs, corners, boxes, fields, read, phi, out):
    me = owner_ref[0]
    owners, depth, _ = read.shape
    own = phi[...].astype(jnp.float32)
    for owner in range(owners):
        rows = slice(owner * depth, (owner + 1) * depth)
        out[rows, :] = read[owner] * own[rows, :]

    def step(row, carry):
        first, second = pairs[row, 0], pairs[row, 1]
        dy = corners[second, 0] - corners[first, 0]
        dx = corners[second, 1] - corners[first, 1]

        @pl.when(first == me)
        def _():
            moved = slide(boxes[second].astype(jnp.float32), dy, dx, side)
            out[...] -= MIXING * fields[row] * moved

        @pl.when(second == me)
        def _():
            product = fields[row] * boxes[first].astype(jnp.float32)
            out[...] -= MIXING * slide(product, -dy, -dx, side)

        return carry

    lax.fori_loop(0, pairs.shape[0], step, 0)


def local_call(kernel, shape, scalars, arrays, name):
    return pl.pallas_call(
        kernel,
        out_shape=jax.ShapeDtypeStruct(shape, jnp.float32),
        in_specs=[pl.BlockSpec(memory_space=pltpu.SMEM)] * len(scalars)
        + [pl.BlockSpec(memory_space=VMEM)] * len(arrays),
        out_specs=pl.BlockSpec(memory_space=VMEM),
        name=name,
    )(*scalars, *arrays)


def body(owners, groups, orbitals, offsets, pairs, ext_pot):
    owner = lax.axis_index("own")
    _, levels, cells = orbitals.shape
    side = side_of(cells)
    grid = side_of(ext_pot.shape[1])
    depth = levels // owners
    padded = jnp.pad(offsets, ((0, 7), (0, 126)))
    boxes, spread = relay(owners, 0, (orbitals[0], padded))
    corners = spread[:, 0, :2]
    scalars = (owner.reshape(1), pairs, corners)

    planes = lax.dynamic_slice_in_dim(boxes, owner * depth, depth, 1).astype(jnp.float32)
    planes = planes.reshape(owners, depth, side, side)
    along_rows = placer(corners[:, 0], grid, side)
    along_cols = placer(corners[:, 1], grid, side)
    partial = jnp.einsum("izyx,ihx->izyh", planes * planes, along_cols, precision=PRECISE)
    partial = jnp.einsum("igy,izyh->zgh", along_rows, partial, precision=PRECISE)
    partial = partial.reshape(depth, grid * grid)
    density = partial
    for step in range(1, groups):
        density = density + lax.ppermute(partial, "grp", [(g, (g + step) % groups) for g in range(groups)])

    each = pairs.shape[0] // owners
    rho = local_call(
        functools.partial(pair_kernel, each, side), (each, levels, cells), scalars, (boxes,), "pair_density"
    )
    green = green_table(levels, side) * (1.0 / float(8 * levels * cells))
    along_z = cas_table(2 * levels, levels)
    along_y = cas_table(2 * side, side)
    fields = []
    for turn in range(each):
        value = rotate("kz,zc->kc", along_z, rho[turn]).reshape(2 * levels, side, side)
        value = rotate("ky,zyx->zkx", along_y, value)
        value = rotate("kx,zyx->zyk", along_y, value)
        value = value * green
        value = rotate("kx,zyk->zyx", along_y, value)
        value = rotate("ky,zkx->zyx", along_y, value).reshape(2 * levels, cells)
        fields.append(rotate("kz,kc->zc", along_z, value))
    field = jnp.concatenate(fields) if each > 1 else fields[0]

    external = lax.dynamic_slice_in_dim(ext_pot, owner * depth, depth, 0)
    potential = external.astype(jnp.float32) - EXCHANGE_COEF * jnp.cbrt(density)
    potential = potential.reshape(depth, grid, grid)
    read = jnp.einsum("igy,zgh->izyh", along_rows, potential, precision=PRECISE)
    read = jnp.einsum("izyh,ihx->izyx", read, along_cols, precision=PRECISE)
    read = read.reshape(owners, depth, cells)
    every, landed = relay(owners, 1, (field,), (read,))
    every = every.reshape(owners * each, levels, cells)
    gradient = local_call(
        functools.partial(combine_kernel, side),
        (levels, cells),
        scalars,
        (boxes, every, landed, orbitals[0]),
        "combine",
    )
    return gradient[None]


def solution(mesh):
    in_specs = (P(("grp", "own"), None, None), P(("grp", "own"), None), P("grp", None), P())
    out_specs = P(("grp", "own"), None, None)
    run = functools.partial(body, mesh.shape["own"], mesh.shape["grp"])
    return jax.shard_map(run, mesh=mesh, in_specs=in_specs, out_specs=out_specs, check_vma=False)
```

time: 102 us -> 80.3 us (0.79)
  the two profiles are of different devices: /device:TPU:15 before, /device:TPU:0 now
where the time goes in v1:
time: 80.3 us; the launch traced here: 79.8 us
  Pallas kernels  49.7 us (62%)
  matrix products  19 us (24%)
  local copies, waits for them, and re-layouts  7.18 us (9%)
  other arithmetic  2.01 us (3%)
  starting transfers between devices  1.76 us (2%)
    pallas_call x2, Pallas kernels, relay(): pl.pallas_call(functools.partial(relay_kernel, count, pieces, exchanged),...  45.3 us
    dot_general x6, matrix products, rotate(): jnp.einsum(pattern, matrix, operand, precision=PRECISE, preferred_element...  17.2 us
    pallas_call x2, Pallas kernels, local_call(): pl.pallas_call(kernel, out_shape=jax.ShapeDtypeStruct(shape, jnp.float32)...  4.33 us
    dot_general x2, local copies, waits for them, and re-layouts, rotate(): jnp.einsum(pattern, matrix, operand, precision=PRECISE, preferred_element...  2 us
    ppermute x3, starting transfers between devices, body(): lax.ppermute(partial, 'grp', [(g, (g + step) % groups) for g in range(gro...  1.76 us
  transfers between devices with their start and end apart: 3, of which 0 were waited for; matrix products, arithmetic and copies ran while one was open for 26% of the time, Pallas kernels for 2%

profile of v1, /device:TPU:0, one launch (start us, length us, event | category | flops | bytes accessed | tf_op | source)
XLA Modules:
  0.0 79.8 jit_solution(9480609301767558900)
XLA Ops:
  0.0 1.3 %pad.4.refs_1_ = s32[8,128]{1,0:T(8,128)} pad(s32[1,2]{1,0:T(1,128)} %param.5, s32[]{:T(128)} %constant.14.clone.1), padding=0_7x0_126 | pad | bytes 4108 | tf_op jit(solution)/shard_map/jit(_pad)/pad | solution.py:292
  1.3 21.1 %relay.2 = (bf16[8,32,1024]{2,1,0:T(8,128)(2,1)}, s32[8,8,128]{2,1,0:T(8,128)}) custom-call(bf16[32,1024]{1,0:T(8,128)(2,1)} %bitcast.60, s32[8,128]{1,0:T(8,128)} %pad.4.refs_1_), custom_call_target="tpu_custom_call" | custom-call | tf_op jit(solution)/shard_map/relay/pallas_call | solution.py:210
  22.4 0.8 slice.9
  23.3 0.9 %convert_multiply_fusion = f32[8,4,1024]{2,1,0:T(4,128)S(1)} fusion(bf16[8,32,1024]{2,1,0:T(8,128)(2,1)} %get-tuple-element.10.boxes, s32[]{:T(128)S(6)} %select_n.42), kind=kLoop, calls=%fused_computation.26 | loop fusion | flops 65536 | bytes 196612 | tf_op jit(solution)/shard_map/mul | solution.py:301
  24.4 0.4 fusion.12
  24.8 0.6 convolution_bitcast_fusion.3
  25.7 1.6 %collective-permute-start.1 = (f32[4,4096]{1,0:T(4,128)S(1)}, f32[4,4096]{1,0:T(4,128)S(1)}, u32[]{:S(2)}, u32[]{:S(2)}) collective-permute-start(f32[4,4096]{1,0:T(4,128)S(1)} %reshape.88), channel_id=1, source_target_pairs={{0,16},{8,24},{16,0},{24,8},{1,17},{9,25},{17,1},{25,9},{2,18},{10... | collective-permute-start | bytes 196616 | tf_op jit(solution)/shard_map/ppermute | solution.py:306
  27.4 0.7 copy.16.corners
  28.1 0.7 copy.15.pairs
  28.8 1.8 %pair_density.1 = f32[1,32,1024]{2,1,0:T(8,128)} custom-call(s32[1]{0:T(128)} %bitcast.owner_ref, s32[8,2]{1,0:T(8,128)} %copy.15.pairs, s32[8,2]{1,0:T(8,128)} %copy.16.corners, bf16[8,32,1024]{2,1,0:T(8,128)(2,1)} %get-tuple-element.10.boxes), custom_call_target="tpu_custom_call" | custom-call | tf_op jit(solution)/shard_map/pair_density/pallas_call | solution.py:276
  30.6 1.1 %dot_general.35 = f32[32,32,32]{1,0,2:T(8,128)S(1)} reshape(f32[1024,32]{0,1:T(8,128)} %bitcast.59) | data formatting | bytes 262144 | tf_op jit(solution)/shard_map/kz,zc->kc/dot_general | solution.py:44
  31.7 1.2 %fusion.14 = f32[64,32,32]{0,2,1:T(8,128)S(1)} fusion(f32[32,32,32]{1,0,2:T(8,128)S(1)} %dot_general.35), kind=kOutput, calls=%fused_computation.18 | convolution fusion | flops 25196544 | bytes 393216 | tf_op jit(solution)/shard_map/kz,zc->kc/dot_general | solution.py:44
  32.9 0.9 %copy.18 = f32[64,32,32]{2,1,0:T(8,128)S(1)} copy(f32[64,32,32]{0,2,1:T(8,128)S(1)} %fusion.14) | data formatting | bytes 524288 | tf_op jit(solution)/shard_map/kz,zc->kc/dot_general | solution.py:44
  33.8 1.8 %convolution_bitcast_fusion = f32[64,64,32]{1,2,0:T(8,128)S(1)} fusion(f32[64,32,32]{2,1,0:T(8,128)S(1)} %copy.18), kind=kOutput, calls=%fused_computation.6 | convolution fusion | flops 50362368 | bytes 786432 | tf_op jit(solution)/shard_map/ky,zyx->zkx/dot_general | solution.py:44
  35.7 3.5 %fusion.34 = f32[64,64,64]{2,1,0:T(8,128)S(1)} fusion(f32[64,64,32]{1,2,0:T(8,128)S(1)} %convolution_bitcast_fusion), kind=kOutput, calls=%fused_computation.41 | convolution fusion | flops 100694016 | bytes 1572864 | tf_op jit(solution)/shard_map/kx,zyx->zyk/dot_general | solution.py:44
  39.2 5.9 %fusion = f32[64,64,32]{1,2,0:T(8,128)S(1)} fusion(f32[64,64,64]{2,1,0:T(8,128)S(1)} %fusion.34, f32[64]{0:T(128)S(1)} %fusion.44, f32[64,64]{1,0:T(8,128)S(1)} %broadcast_add_fusion), kind=kOutput, calls=%fused_computation | convolution fusion | flops 102004736 | bytes 1589504 | tf_op jit(solution)/shard_map/kx,zyk->zyx/dot_general | solution.py:44
  45.2 3.4 %convolution_bitcast_fusion.2 = f32[64,32,32]{0,1,2:T(8,128)S(1)} fusion(f32[64,64,32]{1,2,0:T(8,128)S(1)} %fusion), kind=kOutput, calls=%fused_computation.8 | convolution fusion | flops 50362368 | bytes 786432 | tf_op jit(solution)/shard_map/ky,zkx->zyx/dot_general | solution.py:44
  48.9 1.4 %fusion.41.refs_0_ = f32[32,1024]{1,0:T(8,128)} fusion(f32[64,1024]{0,1:T(8,128)S(1)} %bitcast.58), kind=kOutput, calls=%fused_computation.50 | convolution fusion | flops 25196544 | bytes 393216 | tf_op jit(solution)/shard_map/kz,kc->zc/dot_general | solution.py:44
  50.2 1.0 %multiply_subtract_fusion = f32[4,4096]{1,0:T(4,128)S(1)} fusion(f32[4,4096]{1,0:T(4,128)S(1)} %collective-permute-done.2, f32[4,4096]{1,0:T(4,128)S(1)} %collective-permute-done.1, f32[4,4096]{1,0:T(4,128)S(1)} %reshape.88, f32[4,4096]{1,0:T(4,128)S(1)} %collective-permute-done, bf16[32,4096]{1,0:T(8,128)(2,1)} %param.7, s32[]{:T(128)S(6)} %select_n.42), kind=kLoop, calls=%fused_computation.28 | loop fusion | flops 98304 | bytes 360452 | tf_op jit(solution)/shard_map/sub | solution.py:327
  51.3 0.4 convolution_bitcast_fusion.1
  51.8 0.4 fusion.21
  52.2 0.9 %reshape.90.refs_1_ = f32[8,4,1024]{2,1,0:T(4,128)} reshape(f32[8,4,32,32]{3,2,1,0:T(8,128)S(1)} %fusion.21) | data formatting | bytes 262144 | tf_op jit(solution)/shard_map/reshape | solution.py:331
  53.1 24.2 %relay.3 = (f32[8,32,1024]{2,1,0:T(8,128)}, f32[8,4,1024]{2,1,0:T(4,128)}) custom-call(f32[32,1024]{1,0:T(8,128)} %fusion.41.refs_0_, f32[8,4,1024]{2,1,0:T(4,128)} %reshape.90.refs_1_), custom_call_target="tpu_custom_call" | custom-call | tf_op jit(solution)/shard_map/relay/pallas_call | solution.py:210
  77.3 2.5 %combine.1 = f32[32,1024]{1,0:T(8,128)} custom-call(s32[1]{0:T(128)} %bitcast.owner_ref, s32[8,2]{1,0:T(8,128)} %copy.15.pairs, s32[8,2]{1,0:T(8,128)} %copy.16.corners, bf16[8,32,1024]{2,1,0:T(8,128)(2,1)} %get-tuple-element.10.boxes, f32[8,32,1024]{2,1,0:T(8,128)} %get-tuple-element.11.fields, f32[8,4,1024]{2,1,0:T(4,128)} %get-tuple-element.12.read, ...), custom_call_target="tpu_custom_call" | custom-call | tf_op jit(solution)/shard_map/combine/pallas_call | solution.py:276
  (16 shorter events, 1.2 us)
Async XLA Ops:
  0.0 28.1 %copy-start = (s32[8,2]{0,1:T(2,128)S(1)}, s32[8,2]{0,1:T(2,128)}, u32[]{:S(2)}) copy-start(s32[8,2]{0,1:T(2,128)} %param.6) | copy-start | bytes 196
  25.6 24.6 %collective-permute-start.2 = (f32[4,4096]{1,0:T(4,128)S(1)}, f32[4,4096]{1,0:T(4,128)S(1)}, u32[]{:S(2)}, u32[]{:S(2)}) collective-permute-start(f32[4,4096]{1,0:T(4,128)S(1)} %reshape.88), channel_id=1, source_target_pairs={{0,24},{8,0},{16,8},{24,16},{1,25},{9,1},{17,9},{25,17},{2,26},{10... | collective-permute-start | bytes 196616 | tf_op jit(solution)/shard_map/ppermute | solution.py:306
  25.7 24.5 %collective-permute-start.1 = (f32[4,4096]{1,0:T(4,128)S(1)}, f32[4,4096]{1,0:T(4,128)S(1)}, u32[]{:S(2)}, u32[]{:S(2)}) collective-permute-start(f32[4,4096]{1,0:T(4,128)S(1)} %reshape.88), channel_id=1, source_target_pairs={{0,16},{8,24},{16,0},{24,8},{1,17},{9,25},{17,1},{25,9},{2,18},{10... | collective-permute-start | bytes 196616 | tf_op jit(solution)/shard_map/ppermute | solution.py:306
  27.3 23.0 %collective-permute-start = (f32[4,4096]{1,0:T(4,128)S(1)}, f32[4,4096]{1,0:T(4,128)S(1)}, u32[]{:S(2)}, u32[]{:S(2)}) collective-permute-start(f32[4,4096]{1,0:T(4,128)S(1)} %reshape.88), channel_id=1, source_target_pairs={{0,8},{8,16},{16,24},{24,0},{1,9},{9,17},{17,25},{25,1},{2,10},{10... | collective-permute-start | bytes 196616 | tf_op jit(solution)/shard_map/ppermute | solution.py:306

commit v2 on v1

--- a/solution.py
+++ b/solution.py
@@ -12,6 +12,7 @@
 MIXING = 0.25
 EXCHANGE_COEF = (3.0 / math.pi) ** (1.0 / 3.0)
 PRECISE = lax.Precision.HIGHEST
+SPLIT = lax.Precision.HIGH
 VMEM = pltpu.VMEM
 
 
@@ -41,7 +42,7 @@
 
 
 def rotate(pattern, matrix, operand):
-    return jnp.einsum(pattern, matrix, operand, precision=PRECISE, preferred_element_type=jnp.float32)
+    return jnp.einsum(pattern, matrix, operand, precision=SPLIT, preferred_element_type=jnp.float32)
 
 
 def placer(starts, row_count, side):
@@ -87,8 +88,9 @@
     for piece, source in enumerate(sources):
         rows = source.shape[0]
         if piece == 0:
-            parts.append((piece, 0, rows // 2, False))
-            parts.append((piece, rows // 2, rows // 2, True))
+            front = rows // 2 if source.dtype == jnp.bfloat16 else rows // 4
+            parts.append((piece, 0, front, False))
+            parts.append((piece, front, rows - front, True))
         else:
             parts.append((piece, 0, rows, True))
     fronts = [i for i, part in enumerate(parts) if not part[3]]
@@ -317,7 +319,7 @@
         value = rotate("kz,zc->kc", along_z, rho[turn]).reshape(2 * levels, side, side)
         value = rotate("ky,zyx->zkx", along_y, value)
         value = rotate("kx,zyx->zyk", along_y, value)
-        value = value * green
+        value = lax.optimization_barrier(value * green)
         value = rotate("kx,zyk->zyx", along_y, value)
         value = rotate("ky,zkx->zyx", along_y, value).reshape(2 * levels, cells)
         fields.append(rotate("kz,kc->zc", along_z, value))

time: 80.3 us -> 73 us (0.909)
  matrix products: 19 us -> 11.8 us
    dot_general x6, matrix products: 17.2 us -> 9.97 us  [rotate(): jnp.einsum(pattern, matrix, operand, precision=SPLIT, preferred_element_t...]
  transfers between devices with their start and end apart: 3 -> 3, of which waited for: 0 -> 0; matrix products, arithmetic and copies ran while one was open for 26% -> 19% of each run, Pallas kernels for 2% -> 3%
where the time goes in v2:
time: 73 us
  Pallas kernels  50 us (68%)
  matrix products  11.8 us (16%)
  local copies, waits for them, and re-layouts  7.18 us (10%)
  other arithmetic  2.01 us (3%)
  starting transfers between devices  1.76 us (2%)
    pallas_call x2, Pallas kernels, relay(): pl.pallas_call(functools.partial(relay_kernel, count, pieces, exchanged),...  45.3 us
    dot_general x6, matrix products, rotate(): jnp.einsum(pattern, matrix, operand, precision=SPLIT, preferred_element_t...  9.97 us
    pallas_call x2, Pallas kernels, local_call(): pl.pallas_call(kernel, out_shape=jax.ShapeDtypeStruct(shape, jnp.float32)...  4.72 us
    dot_general x2, local copies, waits for them, and re-layouts, rotate(): jnp.einsum(pattern, matrix, operand, precision=SPLIT, preferred_element_t...  2 us
    ppermute x3, starting transfers between devices, body(): lax.ppermute(partial, 'grp', [(g, (g + step) % groups) for g in range(gro...  1.76 us
  transfers between devices with their start and end apart: 3, of which 0 were waited for; matrix products, arithmetic and copies ran while one was open for 19% of the time, Pallas kernels for 3%

profile of v2, /device:TPU:0, one launch (start us, length us, event | category | flops | bytes accessed | tf_op | source)
XLA Modules:
  0.0 73.0 jit_solution(943637144706490764)
XLA Ops:
  0.0 1.3 %pad.4.refs_1_ = s32[8,128]{1,0:T(8,128)} pad(s32[1,2]{1,0:T(1,128)} %param.5, s32[]{:T(128)} %constant.14.clone.1), padding=0_7x0_126 | pad | bytes 4108 | tf_op jit(solution)/shard_map/jit(_pad)/pad | solution.py:294
  1.3 21.1 %relay.2 = (bf16[8,32,1024]{2,1,0:T(8,128)(2,1)}, s32[8,8,128]{2,1,0:T(8,128)}) custom-call(bf16[32,1024]{1,0:T(8,128)(2,1)} %bitcast.61, s32[8,128]{1,0:T(8,128)} %pad.4.refs_1_), custom_call_target="tpu_custom_call" | custom-call | tf_op jit(solution)/shard_map/relay/pallas_call | solution.py:212
  22.4 0.8 %slice.9 = s32[8,1,2]{2,1,0:T(1,128)S(1)} slice(s32[8,8,128]{2,1,0:T(8,128)} %get-tuple-element.9), slice={[0:8], [0:1], [0:2]} | slice | bytes 128 | tf_op jit(solution)/shard_map/slice | solution.py:296
  23.3 0.9 %convert_multiply_fusion = f32[8,4,1024]{2,1,0:T(4,128)S(1)} fusion(bf16[8,32,1024]{2,1,0:T(8,128)(2,1)} %get-tuple-element.10.boxes, s32[]{:T(128)S(6)} %select_n.42), kind=kLoop, calls=%fused_computation.16 | loop fusion | flops 65536 | bytes 196612 | tf_op jit(solution)/shard_map/mul | solution.py:303
  24.4 0.4 fusion.1
  24.8 0.6 convolution_bitcast_fusion.3
  25.7 1.6 %collective-permute-start.1 = (f32[4,4096]{1,0:T(4,128)S(1)}, f32[4,4096]{1,0:T(4,128)S(1)}, u32[]{:S(2)}, u32[]{:S(2)}) collective-permute-start(f32[4,4096]{1,0:T(4,128)S(1)} %reshape.88), channel_id=1, source_target_pairs={{0,16},{8,24},{16,0},{24,8},{1,17},{9,25},{17,1},{25,9},{2,18},{10... | collective-permute-start | bytes 196616 | tf_op jit(solution)/shard_map/ppermute | solution.py:308
  27.4 0.7 copy.16.corners
  28.1 0.7 copy.15.pairs
  28.8 1.8 %pair_density.1 = f32[1,32,1024]{2,1,0:T(8,128)} custom-call(s32[1]{0:T(128)} %bitcast.owner_ref, s32[8,2]{1,0:T(8,128)} %copy.15.pairs, s32[8,2]{1,0:T(8,128)} %copy.16.corners, bf16[8,32,1024]{2,1,0:T(8,128)(2,1)} %get-tuple-element.10.boxes), custom_call_target="tpu_custom_call" | custom-call | tf_op jit(solution)/shard_map/pair_density/pallas_call | solution.py:278
  30.6 1.1 %dot_general.35 = f32[32,32,32]{1,0,2:T(8,128)S(1)} reshape(f32[1024,32]{0,1:T(8,128)} %bitcast.60) | data formatting | bytes 262144 | tf_op jit(solution)/shard_map/kz,zc->kc/dot_general | solution.py:45
  31.7 0.8 %fusion.3 = f32[64,32,32]{0,2,1:T(8,128)S(1)} fusion(f32[32,32,32]{1,0,2:T(8,128)S(1)} %dot_general.35), kind=kOutput, calls=%fused_computation.8 | convolution fusion | flops 12613632 | bytes 393216 | tf_op jit(solution)/shard_map/kz,zc->kc/dot_general | solution.py:45
  32.5 0.9 %copy.18 = f32[64,32,32]{2,1,0:T(8,128)S(1)} copy(f32[64,32,32]{0,2,1:T(8,128)S(1)} %fusion.3) | data formatting | bytes 524288 | tf_op jit(solution)/shard_map/kz,zc->kc/dot_general | solution.py:45
  33.4 1.0 %convolution_bitcast_fusion = f32[64,64,32]{1,2,0:T(8,128)S(1)} fusion(f32[64,32,32]{2,1,0:T(8,128)S(1)} %copy.18), kind=kOutput, calls=%fused_computation.1 | convolution fusion | flops 25196544 | bytes 786432 | tf_op jit(solution)/shard_map/ky,zyx->zkx/dot_general | solution.py:45
  34.5 2.3 %multiply_multiply_fusion = f32[64,64,64]{2,1,0:T(8,128)S(1)} fusion(f32[64,64,32]{1,2,0:T(8,128)S(1)} %convolution_bitcast_fusion, f32[64]{0:T(128)S(1)} %fusion.33, f32[64,64]{1,0:T(8,128)S(1)} %broadcast_add_fusion), kind=kOutput, calls=%fused_computation | convolution fusion | flops 51673088 | bytes 1589504 | tf_op jit(solution)/shard_map/kx,zyx->zyk/dot_general | solution.py:45
  36.8 3.0 %fusion.22 = f32[64,64,32]{1,2,0:T(8,128)S(1)} fusion(f32[64,64,64]{2,1,0:T(8,128)S(1)} %multiply_multiply_fusion), kind=kOutput, calls=%fused_computation.30 | convolution fusion | flops 50362368 | bytes 1572864 | tf_op jit(solution)/shard_map/kx,zyk->zyx/dot_general | solution.py:45
  39.8 1.8 %convolution_bitcast_fusion.2 = f32[64,32,32]{0,1,2:T(8,128)S(1)} fusion(f32[64,64,32]{1,2,0:T(8,128)S(1)} %fusion.22), kind=kOutput, calls=%fused_computation.3 | convolution fusion | flops 25196544 | bytes 786432 | tf_op jit(solution)/shard_map/ky,zkx->zyx/dot_general | solution.py:45
  41.9 1.1 %fusion.30.refs_0_ = f32[32,1024]{1,0:T(8,128)} fusion(f32[64,1024]{0,1:T(8,128)S(1)} %bitcast.59), kind=kOutput, calls=%fused_computation.40 | convolution fusion | flops 12613632 | bytes 393216 | tf_op jit(solution)/shard_map/kz,kc->zc/dot_general | solution.py:45
  43.0 1.0 %multiply_subtract_fusion = f32[4,4096]{1,0:T(4,128)S(1)} fusion(f32[4,4096]{1,0:T(4,128)S(1)} %collective-permute-done.2, f32[4,4096]{1,0:T(4,128)S(1)} %collective-permute-done.1, f32[4,4096]{1,0:T(4,128)S(1)} %reshape.88, f32[4,4096]{1,0:T(4,128)S(1)} %collective-permute-done, bf16[32,4096]{1,0:T(8,128)(2,1)} %param.7, s32[]{:T(128)S(6)} %select_n.42), kind=kLoop, calls=%fused_computation.18 | loop fusion | flops 98304 | bytes 360452 | tf_op jit(solution)/shard_map/sub | solution.py:329
  44.1 0.4 convolution_bitcast_fusion.1
  44.5 0.4 fusion.10
  45.0 0.9 %reshape.90.refs_1_ = f32[8,4,1024]{2,1,0:T(4,128)} reshape(f32[8,4,32,32]{3,2,1,0:T(8,128)S(1)} %fusion.10) | data formatting | bytes 262144 | tf_op jit(solution)/shard_map/reshape | solution.py:333
  45.9 24.2 %relay.3 = (f32[8,32,1024]{2,1,0:T(8,128)}, f32[8,4,1024]{2,1,0:T(4,128)}) custom-call(f32[32,1024]{1,0:T(8,128)} %fusion.30.refs_0_, f32[8,4,1024]{2,1,0:T(4,128)} %reshape.90.refs_1_), custom_call_target="tpu_custom_call" | custom-call | tf_op jit(solution)/shard_map/relay/pallas_call | solution.py:212
  70.1 2.9 %combine.1 = f32[32,1024]{1,0:T(8,128)} custom-call(s32[1]{0:T(128)} %bitcast.owner_ref, s32[8,2]{1,0:T(8,128)} %copy.15.pairs, s32[8,2]{1,0:T(8,128)} %copy.16.corners, bf16[8,32,1024]{2,1,0:T(8,128)(2,1)} %get-tuple-element.10.boxes, f32[8,32,1024]{2,1,0:T(8,128)} %get-tuple-element.11.fields, f32[8,4,1024]{2,1,0:T(4,128)} %get-tuple-element.12.read, ...), custom_call_target="tpu_custom_call" | custom-call | tf_op jit(solution)/shard_map/combine/pallas_call | solution.py:278
  (16 shorter events, 1.2 us)
Async XLA Ops:
  0.0 28.1 %copy-start = (s32[8,2]{0,1:T(2,128)S(1)}, s32[8,2]{0,1:T(2,128)}, u32[]{:S(2)}) copy-start(s32[8,2]{0,1:T(2,128)} %param.6) | copy-start | bytes 196
  25.6 17.4 %collective-permute-start.2 = (f32[4,4096]{1,0:T(4,128)S(1)}, f32[4,4096]{1,0:T(4,128)S(1)}, u32[]{:S(2)}, u32[]{:S(2)}) collective-permute-start(f32[4,4096]{1,0:T(4,128)S(1)} %reshape.88), channel_id=1, source_target_pairs={{0,24},{8,0},{16,8},{24,16},{1,25},{9,1},{17,9},{25,17},{2,26},{10... | collective-permute-start | bytes 196616 | tf_op jit(solution)/shard_map/ppermute | solution.py:308
  25.7 17.3 %collective-permute-start.1 = (f32[4,4096]{1,0:T(4,128)S(1)}, f32[4,4096]{1,0:T(4,128)S(1)}, u32[]{:S(2)}, u32[]{:S(2)}) collective-permute-start(f32[4,4096]{1,0:T(4,128)S(1)} %reshape.88), channel_id=1, source_target_pairs={{0,16},{8,24},{16,0},{24,8},{1,17},{9,25},{17,1},{25,9},{2,18},{10... | collective-permute-start | bytes 196616 | tf_op jit(solution)/shard_map/ppermute | solution.py:308
  27.3 15.7 %collective-permute-start = (f32[4,4096]{1,0:T(4,128)S(1)}, f32[4,4096]{1,0:T(4,128)S(1)}, u32[]{:S(2)}, u32[]{:S(2)}) collective-permute-start(f32[4,4096]{1,0:T(4,128)S(1)} %reshape.88), channel_id=1, source_target_pairs={{0,8},{8,16},{16,24},{24,0},{1,9},{9,17},{17,25},{25,1},{2,10},{10... | collective-permute-start | bytes 196616 | tf_op jit(solution)/shard_map/ppermute | solution.py:308

commit v3 on v2

--- a/solution.py
+++ b/solution.py
@@ -54,6 +54,13 @@
 def plane_split(count):
     rows = 1 << ((count.bit_length() - 1) // 2)
     return count // rows, rows
+
+
+def chunk_rows(array):
+    rows = array.shape[0]
+    if rows <= 8:
+        return rows
+    return rows // 2 if array.dtype == jnp.bfloat16 else rows // 4
 
 
 def relay_kernel(count, pieces, exchanged, *refs):
@@ -87,12 +94,9 @@
     parts = []
     for piece, source in enumerate(sources):
         rows = source.shape[0]
-        if piece == 0:
-            front = rows // 2 if source.dtype == jnp.bfloat16 else rows // 4
-            parts.append((piece, 0, front, False))
-            parts.append((piece, front, rows - front, True))
-        else:
-            parts.append((piece, 0, rows, True))
+        size = chunk_rows(source)
+        for start_row in range(0, rows, size):
+            parts.append((piece, start_row, size, piece > 0 or start_row > 0))
     fronts = [i for i, part in enumerate(parts) if not part[3]]
     backs = [i for i, part in enumerate(parts) if part[3]]
 
@@ -143,11 +147,11 @@
         sideways(index, me, True, start)
     for index in backs:
         sideways(index, me, True, start)
+    for index in fronts:
+        both(index, me, True, start)
     for index in range(exchanged):
         for step in range(1, count):
             slab_copy(index, step).start()
-    for index in fronts:
-        both(index, me, True, start)
     locals_ = [
         pltpu.make_async_copy(sources[piece], targets[piece].at[me], local_sem.at[piece]) for piece in range(pieces)
     ]
@@ -206,6 +210,7 @@
 
 def relay(count, collective_id, arrays, slabs=()):
     pieces, exchanged = len(arrays), len(slabs)
+    parts = sum(a.shape[0] // chunk_rows(a) for a in arrays)
     _, near = plane_split(count)
     shapes = [jax.ShapeDtypeStruct((count,) + a.shape, a.dtype) for a in arrays]
     shapes += [jax.ShapeDtypeStruct(a.shape, a.dtype) for a in slabs]
@@ -215,8 +220,8 @@
         in_specs=[pl.BlockSpec(memory_space=VMEM)] * (pieces + exchanged),
         out_specs=[pl.BlockSpec(memory_space=VMEM)] * (pieces + exchanged),
         scratch_shapes=[
-            pltpu.SemaphoreType.DMA((pieces + 1, count, near + 1)),
-            pltpu.SemaphoreType.DMA((pieces + 1, count)),
+            pltpu.SemaphoreType.DMA((parts, count, near + 1)),
+            pltpu.SemaphoreType.DMA((parts, count)),
             pltpu.SemaphoreType.DMA((pieces + exchanged,)),
             pltpu.SemaphoreType.DMA((max(exchanged, 1), count)),
             pltpu.SemaphoreType.DMA((max(exchanged, 1), count)),

time: 73 us -> 72 us (0.986)
  Pallas kernels: 50 us -> 49 us
    pallas_call x2, Pallas kernels: 45.3 us -> 44.5 us  [relay(): pl.pallas_call(functools.partial(relay_kernel, count, pieces, exchanged),...]
where the time goes in v3:
time: 72 us; the launch traced here: 71.9 us
  Pallas kernels  49 us (68%)
  matrix products  11.8 us (16%)
  local copies, waits for them, and re-layouts  7.18 us (10%)
  other arithmetic  2.01 us (3%)
  starting transfers between devices  1.76 us (2%)
    pallas_call x2, Pallas kernels, relay(): pl.pallas_call(functools.partial(relay_kernel, count, pieces, exchanged),...  44.5 us
    dot_general x6, matrix products, rotate(): jnp.einsum(pattern, matrix, operand, precision=SPLIT, preferred_element_t...  9.97 us
    pallas_call x2, Pallas kernels, local_call(): pl.pallas_call(kernel, out_shape=jax.ShapeDtypeStruct(shape, jnp.float32)...  4.46 us
    dot_general x2, local copies, waits for them, and re-layouts, rotate(): jnp.einsum(pattern, matrix, operand, precision=SPLIT, preferred_element_t...  2 us
    ppermute x3, starting transfers between devices, body(): lax.ppermute(partial, 'grp', [(g, (g + step) % groups) for g in range(gro...  1.76 us
  transfers between devices with their start and end apart: 3, of which 0 were waited for; matrix products, arithmetic and copies ran while one was open for 19% of the time, Pallas kernels for 3%

profile of v3, /device:TPU:0, one launch (start us, length us, event | category | flops | bytes accessed | tf_op | source)
XLA Modules:
  0.0 71.9 jit_solution(4953594313291604326)
XLA Ops:
  0.0 1.3 %pad.4.refs_1_ = s32[8,128]{1,0:T(8,128)} pad(s32[1,2]{1,0:T(1,128)} %param.5, s32[]{:T(128)} %constant.14.clone.1), padding=0_7x0_126 | pad | bytes 4108 | tf_op jit(solution)/shard_map/jit(_pad)/pad | solution.py:299
  1.3 21.1 %relay.2 = (bf16[8,32,1024]{2,1,0:T(8,128)(2,1)}, s32[8,8,128]{2,1,0:T(8,128)}) custom-call(bf16[32,1024]{1,0:T(8,128)(2,1)} %bitcast.61, s32[8,128]{1,0:T(8,128)} %pad.4.refs_1_), custom_call_target="tpu_custom_call" | custom-call | tf_op jit(solution)/shard_map/relay/pallas_call | solution.py:217
  22.4 0.8 %slice.9 = s32[8,1,2]{2,1,0:T(1,128)S(1)} slice(s32[8,8,128]{2,1,0:T(8,128)} %get-tuple-element.9), slice={[0:8], [0:1], [0:2]} | slice | bytes 128 | tf_op jit(solution)/shard_map/slice | solution.py:301
  23.3 0.9 %convert_multiply_fusion = f32[8,4,1024]{2,1,0:T(4,128)S(1)} fusion(bf16[8,32,1024]{2,1,0:T(8,128)(2,1)} %get-tuple-element.10.boxes, s32[]{:T(128)S(6)} %select_n.42), kind=kLoop, calls=%fused_computation.16 | loop fusion | flops 65536 | bytes 196612 | tf_op jit(solution)/shard_map/mul | solution.py:308
  24.4 0.4 fusion.1
  24.8 0.6 convolution_bitcast_fusion.3
  25.7 1.6 %collective-permute-start.1 = (f32[4,4096]{1,0:T(4,128)S(1)}, f32[4,4096]{1,0:T(4,128)S(1)}, u32[]{:S(2)}, u32[]{:S(2)}) collective-permute-start(f32[4,4096]{1,0:T(4,128)S(1)} %reshape.88), channel_id=1, source_target_pairs={{0,16},{8,24},{16,0},{24,8},{1,17},{9,25},{17,1},{25,9},{2,18},{10... | collective-permute-start | bytes 196616 | tf_op jit(solution)/shard_map/ppermute | solution.py:313
  27.4 0.7 copy.16.corners
  28.1 0.7 copy.15.pairs
  28.8 1.8 %pair_density.1 = f32[1,32,1024]{2,1,0:T(8,128)} custom-call(s32[1]{0:T(128)} %bitcast.owner_ref, s32[8,2]{1,0:T(8,128)} %copy.15.pairs, s32[8,2]{1,0:T(8,128)} %copy.16.corners, bf16[8,32,1024]{2,1,0:T(8,128)(2,1)} %get-tuple-element.10.boxes), custom_call_target="tpu_custom_call" | custom-call | tf_op jit(solution)/shard_map/pair_density/pallas_call | solution.py:283
  30.6 1.1 %dot_general.35 = f32[32,32,32]{1,0,2:T(8,128)S(1)} reshape(f32[1024,32]{0,1:T(8,128)} %bitcast.60) | data formatting | bytes 262144 | tf_op jit(solution)/shard_map/kz,zc->kc/dot_general | solution.py:45
  31.7 0.8 %fusion.3 = f32[64,32,32]{0,2,1:T(8,128)S(1)} fusion(f32[32,32,32]{1,0,2:T(8,128)S(1)} %dot_general.35), kind=kOutput, calls=%fused_computation.8 | convolution fusion | flops 12613632 | bytes 393216 | tf_op jit(solution)/shard_map/kz,zc->kc/dot_general | solution.py:45
  32.5 0.9 %copy.18 = f32[64,32,32]{2,1,0:T(8,128)S(1)} copy(f32[64,32,32]{0,2,1:T(8,128)S(1)} %fusion.3) | data formatting | bytes 524288 | tf_op jit(solution)/shard_map/kz,zc->kc/dot_general | solution.py:45
  33.4 1.0 %convolution_bitcast_fusion = f32[64,64,32]{1,2,0:T(8,128)S(1)} fusion(f32[64,32,32]{2,1,0:T(8,128)S(1)} %copy.18), kind=kOutput, calls=%fused_computation.1 | convolution fusion | flops 25196544 | bytes 786432 | tf_op jit(solution)/shard_map/ky,zyx->zkx/dot_general | solution.py:45
  34.5 2.3 %multiply_multiply_fusion = f32[64,64,64]{2,1,0:T(8,128)S(1)} fusion(f32[64,64,32]{1,2,0:T(8,128)S(1)} %convolution_bitcast_fusion, f32[64]{0:T(128)S(1)} %fusion.33, f32[64,64]{1,0:T(8,128)S(1)} %broadcast_add_fusion), kind=kOutput, calls=%fused_computation | convolution fusion | flops 51673088 | bytes 1589504 | tf_op jit(solution)/shard_map/kx,zyx->zyk/dot_general | solution.py:45
  36.8 3.0 %fusion.22 = f32[64,64,32]{1,2,0:T(8,128)S(1)} fusion(f32[64,64,64]{2,1,0:T(8,128)S(1)} %multiply_multiply_fusion), kind=kOutput, calls=%fused_computation.30 | convolution fusion | flops 50362368 | bytes 1572864 | tf_op jit(solution)/shard_map/kx,zyk->zyx/dot_general | solution.py:45
  39.8 1.8 %convolution_bitcast_fusion.2 = f32[64,32,32]{0,1,2:T(8,128)S(1)} fusion(f32[64,64,32]{1,2,0:T(8,128)S(1)} %fusion.22), kind=kOutput, calls=%fused_computation.3 | convolution fusion | flops 25196544 | bytes 786432 | tf_op jit(solution)/shard_map/ky,zkx->zyx/dot_general | solution.py:45
  41.9 1.1 %fusion.30.refs_0_ = f32[32,1024]{1,0:T(8,128)} fusion(f32[64,1024]{0,1:T(8,128)S(1)} %bitcast.59), kind=kOutput, calls=%fused_computation.40 | convolution fusion | flops 12613632 | bytes 393216 | tf_op jit(solution)/shard_map/kz,kc->zc/dot_general | solution.py:45
  43.0 1.0 %multiply_subtract_fusion = f32[4,4096]{1,0:T(4,128)S(1)} fusion(f32[4,4096]{1,0:T(4,128)S(1)} %collective-permute-done.2, f32[4,4096]{1,0:T(4,128)S(1)} %collective-permute-done.1, f32[4,4096]{1,0:T(4,128)S(1)} %reshape.88, f32[4,4096]{1,0:T(4,128)S(1)} %collective-permute-done, bf16[32,4096]{1,0:T(8,128)(2,1)} %param.7, s32[]{:T(128)S(6)} %select_n.42), kind=kLoop, calls=%fused_computation.18 | loop fusion | flops 98304 | bytes 360452 | tf_op jit(solution)/shard_map/sub | solution.py:334
  44.1 0.4 convolution_bitcast_fusion.1
  44.5 0.4 fusion.10
  45.0 0.9 %reshape.90.refs_1_ = f32[8,4,1024]{2,1,0:T(4,128)} reshape(f32[8,4,32,32]{3,2,1,0:T(8,128)S(1)} %fusion.10) | data formatting | bytes 262144 | tf_op jit(solution)/shard_map/reshape | solution.py:338
  45.9 23.4 %relay.3 = (f32[8,32,1024]{2,1,0:T(8,128)}, f32[8,4,1024]{2,1,0:T(4,128)}) custom-call(f32[32,1024]{1,0:T(8,128)} %fusion.30.refs_0_, f32[8,4,1024]{2,1,0:T(4,128)} %reshape.90.refs_1_), custom_call_target="tpu_custom_call" | custom-call | tf_op jit(solution)/shard_map/relay/pallas_call | solution.py:217
  69.3 2.6 %combine.1 = f32[32,1024]{1,0:T(8,128)} custom-call(s32[1]{0:T(128)} %bitcast.owner_ref, s32[8,2]{1,0:T(8,128)} %copy.15.pairs, s32[8,2]{1,0:T(8,128)} %copy.16.corners, bf16[8,32,1024]{2,1,0:T(8,128)(2,1)} %get-tuple-element.10.boxes, f32[8,32,1024]{2,1,0:T(8,128)} %get-tuple-element.11.fields, f32[8,4,1024]{2,1,0:T(4,128)} %get-tuple-element.12.read, ...), custom_call_target="tpu_custom_call" | custom-call | tf_op jit(solution)/shard_map/combine/pallas_call | solution.py:283
  (16 shorter events, 1.2 us)
Async XLA Ops:
  0.0 28.1 %copy-start = (s32[8,2]{0,1:T(2,128)S(1)}, s32[8,2]{0,1:T(2,128)}, u32[]{:S(2)}) copy-start(s32[8,2]{0,1:T(2,128)} %param.6) | copy-start | bytes 196
  25.6 17.4 %collective-permute-start.2 = (f32[4,4096]{1,0:T(4,128)S(1)}, f32[4,4096]{1,0:T(4,128)S(1)}, u32[]{:S(2)}, u32[]{:S(2)}) collective-permute-start(f32[4,4096]{1,0:T(4,128)S(1)} %reshape.88), channel_id=1, source_target_pairs={{0,24},{8,0},{16,8},{24,16},{1,25},{9,1},{17,9},{25,17},{2,26},{10... | collective-permute-start | bytes 196616 | tf_op jit(solution)/shard_map/ppermute | solution.py:313
  25.7 17.3 %collective-permute-start.1 = (f32[4,4096]{1,0:T(4,128)S(1)}, f32[4,4096]{1,0:T(4,128)S(1)}, u32[]{:S(2)}, u32[]{:S(2)}) collective-permute-start(f32[4,4096]{1,0:T(4,128)S(1)} %reshape.88), channel_id=1, source_target_pairs={{0,16},{8,24},{16,0},{24,8},{1,17},{9,25},{17,1},{25,9},{2,18},{10... | collective-permute-start | bytes 196616 | tf_op jit(solution)/shard_map/ppermute | solution.py:313
  27.3 15.7 %collective-permute-start = (f32[4,4096]{1,0:T(4,128)S(1)}, f32[4,4096]{1,0:T(4,128)S(1)}, u32[]{:S(2)}, u32[]{:S(2)}) collective-permute-start(f32[4,4096]{1,0:T(4,128)S(1)} %reshape.88), channel_id=1, source_target_pairs={{0,8},{8,16},{16,24},{24,0},{1,9},{9,17},{17,25},{25,1},{2,10},{10... | collective-permute-start | bytes 196616 | tf_op jit(solution)/shard_map/ppermute | solution.py:313
